TPU v7x, 256 devices: a whole 4x4x8 slice. The times are simulated.
256 devices in a mesh: src: 8 (over y, core), snk: 32 (over x, z).
Axes of the slice: x: 4, y: 4, z: 8, core: 2. Of those that a mesh axis runs over, the one named last changes fastest.
Arguments:
- peram: bfloat16 [8, 32, 2, 256, 256], P('src', None, None, None, 'snk'), may hold values from -6 to 6
- meson_blocks: bfloat16 [32, 4, 2, 256, 256], P('snk'), may hold values from -0.25 to 0.25
- edge_left: int32 [8, 32, 32], P('src', 'snk'), may hold values from 0 to 3
- edge_right: int32 [8, 32, 32], P('src', 'snk'), may hold values from 0 to 3
- edge_node: int32 [8, 32, 32], P('src', 'snk'), may hold values from 0 to 4
- edge_weight: int32 [8, 32, 32], P('src', 'snk'), may hold values from 0 to 15
- weight_table: float32 [16, 2], replicated, may hold values from -0.2 to 0.2
Outputs:
- node_matrices: bfloat16 [256, 4, 2, 256], P('snk')
Inputs may be any that keep to these rules, and one draw needn't show every extreme that they name: `edge_node`: the value 4 marks an empty slot that feeds no node.
All inputs are finite; a program needn't handle non-finite values.
Results may differ from a plain program's by a relative error of at most 0.009.
Values may be sent and summed in bfloat16 or wider, within the bound.
No kernel may reach another device: no remote copies, remote signals or barrier semaphores. Data moves between devices by JAX's collectives and lax.ppermute only.
A program may use at most 128 MiB of HBM per device.

v0:
```python
import jax
import jax.numpy as jnp
from jax import lax
from jax.sharding import PartitionSpec as P

NODES = 4
NW = 16


def from_root(value, axis, source):
    kept = jnp.where(lax.axis_index(axis) == source, value, 0).astype(value.dtype)
    return lax.psum(kept, axis)


def block_products(blocks, whole_peram):
    number = blocks.shape[0]
    order = blocks.shape[2]
    left_real = blocks[:, 0].reshape(number * order, order)
    left_imag = blocks[:, 1].reshape(number * order, order)
    real_part = jnp.dot(left_real, whole_peram[0], preferred_element_type=jnp.float32) - jnp.dot(
        left_imag, whole_peram[1], preferred_element_type=jnp.float32
    )
    imag_part = jnp.dot(left_real, whole_peram[1], preferred_element_type=jnp.float32) + jnp.dot(
        left_imag, whole_peram[0], preferred_element_type=jnp.float32
    )
    stacked = jnp.stack(
        [real_part.reshape(number, order, order), imag_part.reshape(number, order, order)], 1
    )
    return stacked.astype(jnp.bfloat16)


def shards(peram, meson_blocks, edge_left, edge_right, edge_node, edge_weight, weight_table):
    high = lax.Precision.HIGHEST
    src_total = lax.axis_size("src")
    snk_total = lax.axis_size("snk")
    whole_peram = lax.all_to_all(peram, "snk", split_axis=1, concat_axis=4, tiled=True)[0, 0]
    source_root = lax.axis_index("src") * (snk_total // src_total)
    right_all = from_root(meson_blocks, "snk", source_root)[0]
    left_all = meson_blocks[0]
    left_of = edge_left[0, 0]
    right_of = edge_right[0, 0]
    node_of = edge_node[0, 0]
    weight_of = edge_weight[0, 0]
    pick_weight = (weight_of[:, None] == jnp.arange(NW, dtype=jnp.int32)[None, :]).astype(
        jnp.float32
    )
    edge_coef = jnp.dot(pick_weight, weight_table, precision=high)
    member = (node_of[:, None] == jnp.arange(NODES, dtype=jnp.int32)[None, :]).astype(jnp.float32)
    gain_real = member * edge_coef[:, 0:1]
    gain_imag = member * edge_coef[:, 1:2]
    every_block = block_products(left_all, whole_peram)
    left_times = every_block[left_of]
    right_pick = right_all[right_of]
    prod_real = jnp.einsum(
        "eij,ejk->eik", left_times[:, 0], right_pick[:, 0], preferred_element_type=jnp.float32
    ) - jnp.einsum(
        "eij,ejk->eik", left_times[:, 1], right_pick[:, 1], preferred_element_type=jnp.float32
    )
    prod_imag = jnp.einsum(
        "eij,ejk->eik", left_times[:, 0], right_pick[:, 1], preferred_element_type=jnp.float32
    ) + jnp.einsum(
        "eij,ejk->eik", left_times[:, 1], right_pick[:, 0], preferred_element_type=jnp.float32
    )
    term_real = jnp.einsum("en,eik->ink", gain_real, prod_real, precision=high) - jnp.einsum(
        "en,eik->ink", gain_imag, prod_imag, precision=high
    )
    term_imag = jnp.einsum("en,eik->ink", gain_real, prod_imag, precision=high) + jnp.einsum(
        "en,eik->ink", gain_imag, prod_real, precision=high
    )
    node_share = lax.psum_scatter(
        jnp.stack([term_real, term_imag], 2), "snk", scatter_dimension=0, tiled=True
    )
    summed = lax.psum(node_share, "src")
    return summed.astype(jnp.bfloat16)


def solution(mesh):
    return jax.shard_map(
        shards,
        mesh=mesh,
        in_specs=(
            P("src", None, None, None, "snk"),
            P("snk", None, None, None, None),
            P("src", "snk", None),
            P("src", "snk", None),
            P("src", "snk", None),
            P("src", "snk", None),
            P(),
        ),
        out_specs=P("snk", None, None, None),
        check_vma=False,
    )
```

profile of v0, /device:TPU:2, one launch (start us, length us, event | category | flops | bytes accessed | tf_op | source)
XLA Modules:
  0.0 496.3 jit_solution(17414730400957599875)
XLA Ops:
  6.5 0.0 copy-start
  6.5 11.8 %all-to-all-start = ((bf16[1,32,2,256,8]{3,4,2,0,1:T(8,128)(2,1)}), bf16[1,32,2,256,8]{3,4,2,0,1:T(8,128)(2,1)S(1)}, u32[]{:S(2)}, u32[]{:S(2)}) async-start(bf16[1,32,2,256,8]{3,4,2,0,1:T(8,128)(2,1)} %bitcast.109), calls=%async_computation | async-start | bytes 524288 | tf_op jit(solution)/shard_map/all_to_all | solution.py:36
  18.3 0.0 all-reduce.2.cloned.1.call-start
  18.4 1.1 select_bitcast_fusion
  19.4 0.0 all-reduce.2.cloned.1.call-update
  19.4 0.0 reduce-scatter.5.cloned.1.call-start
  19.5 0.7 fusion.52
  20.1 0.7 fusion.53
  20.8 0.0 copy-done
  20.8 0.8 fusion.30
  21.7 1.3 fusion.58
  23.0 6.6 %all-to-all-done = bf16[1,32,2,256,8]{3,4,2,0,1:T(8,128)(2,1)S(1)} async-done(((bf16[1,32,2,256,8]{3,4,2,0,1:T(8,128)(2,1)}), bf16[1,32,2,256,8]{3,4,2,0,1:T(8,128)(2,1)S(1)}, u32[]{:S(2)}, u32[]{:S(2)}) %all-to-all-start) | async-done | bytes 262176 | tf_op jit(solution)/shard_map/all_to_all | solution.py:36
  29.6 0.3 fusion.29
  29.9 0.3 fusion.28
  30.2 0.3 fusion.27
  30.6 0.3 fusion.26
  30.9 0.1 pad_maximum_fusion.1
  31.0 5.1 %gather_fusion = bf16[32,2,256,256]{3,2,1,0:T(8,128)(2,1)} fusion(bf16[4,2,256,256]{3,2,1,0:T(8,128)(2,1)S(1)} %pad_maximum_fusion.1, s32[1024]{0:T(1024)S(1)} %pad_clamp_fusion.1), kind=kCustom, calls=%fused_computation | custom fusion | bytes 16777344 | tf_op jit(solution)/shard_map/gather | solution.py:52
  36.1 136.7 %all-reduce.2.cloned.1.call-done = bf16[4,2,256,256]{3,2,1,0:T(8,128)(2,1)} async-done(((bf16[4,2,256,256]{3,2,1,0:T(8,128)(2,1)}), bf16[4,2,256,256]{3,2,1,0:T(8,128)(2,1)}) %all-reduce.2.cloned.1.call-update) | async-done | bytes 1048592 | tf_op jit(solution)/shard_map/psum | solution.py:12
  172.8 6.6 %gather_fusion.1 = bf16[32,2,256,256]{3,2,1,0:T(8,128)(2,1)} fusion(bf16[4,2,256,256]{3,2,1,0:T(8,128)(2,1)} %all-reduce.2.cloned.1.call-done, s32[1024]{0:T(1024)S(1)} %pad_clamp_fusion), kind=kCustom, calls=%fused_computation.1 | custom fusion | bytes 16777344 | tf_op jit(solution)/shard_map/gather | solution.py:53
  179.4 0.0 copy-start.2
  179.4 0.0 copy-start.3
  179.4 9.1 %fusion.8 = f32[32,256,256]{2,1,0:T(8,128)} fusion(bf16[32,2,256,256]{3,2,1,0:T(8,128)(2,1)} %gather_fusion, bf16[32,2,256,256]{3,2,1,0:T(8,128)(2,1)} %gather_fusion.1), kind=kOutput, calls=%fused_computation.14 | convolution fusion | flops 1073741824 | bytes 16777216 | tf_op jit(solution)/shard_map/eij,ejk->eik/dot_general | solution.py:59
  188.5 0.0 copy-done.2
  188.5 2.1 copy-done.3
  190.7 4.5 fusion.9
  195.2 0.0 copy-start.4
  195.2 5.9 %fusion.13 = f32[32,256,256]{2,1,0:T(8,128)S(1)} fusion(f32[32,256,256]{2,1,0:T(8,128)} %fusion.8, bf16[32,2,256,256]{3,2,1,0:T(8,128)(2,1)} %gather_fusion.1, bf16[32,2,256,256]{3,2,1,0:T(8,128)(2,1)S(1)} %copy-done.2), kind=kOutput, calls=%fused_computation.19 | convolution fusion | flops 1075838976 | bytes 25165824 | tf_op jit(solution)/shard_map/eij,ejk->eik/dot_general | solution.py:61
  201.1 0.0 copy-done.4
  201.1 9.3 %fusion = f32[256,256,4]{1,2,0:T(4,128)S(1)} fusion(f32[32,256,256]{2,1,0:T(8,128)S(1)} %fusion.13, f32[32]{0:T(128)S(1)} %get-tuple-element.8, s32[32]{0:T(128)S(1)} %bitcast.111), kind=kOutput, calls=%fused_computation.2 | convolution fusion | flops 100663552 | bytes 9437440 | tf_op jit(solution)/shard_map/en,eik->ink/dot_general | solution.py:67
  210.4 9.1 %fusion.2 = f32[256,256,4]{1,2,0:T(4,128)S(1)} fusion(f32[32,256,256]{2,1,0:T(8,128)S(1)} %fusion.13, f32[32]{0:T(128)S(1)} %get-tuple-element.7, s32[32]{0:T(128)S(1)} %bitcast.112), kind=kOutput, calls=%fused_computation.4 | convolution fusion | flops 100663552 | bytes 9437440 | tf_op jit(solution)/shard_map/en,eik->ink/dot_general | solution.py:64
  219.5 6.1 %fusion.12 = f32[32,256,256]{2,1,0:T(8,128)S(1)} fusion(f32[32,256,256]{2,1,0:T(8,128)} %fusion.9, bf16[32,2,256,256]{3,2,1,0:T(8,128)(2,1)} %gather_fusion.1, bf16[32,2,256,256]{3,2,1,0:T(8,128)(2,1)S(1)} %copy-done.2), kind=kOutput, calls=%fused_computation.18 | convolution fusion | flops 1075838976 | bytes 25165824 | tf_op jit(solution)/shard_map/eij,ejk->eik/dot_general | solution.py:56
  225.6 0.0 copy-start.1
  225.6 9.1 %fusion.23 = f32[256,4,1,256]{3,1,0,2:T(4,128)S(1)} fusion(f32[256,256,4]{1,2,0:T(4,128)S(1)} %fusion, f32[32,256,256]{2,1,0:T(8,128)S(1)} %fusion.12, f32[32]{0:T(128)S(1)} %get-tuple-element.7, s32[32]{0:T(128)S(1)} %bitcast.113), kind=kOutput, calls=%fused_computation.27 | convolution fusion | flops 100925696 | bytes 10486016 | tf_op jit(solution)/shard_map/en,eik->ink/dot_general | solution.py:67
  234.8 9.4 %fusion.17 = f32[256,4,1,256]{3,1,0,2:T(4,128)S(1)} fusion(f32[256,256,4]{1,2,0:T(4,128)S(1)} %fusion.2, f32[32,256,256]{2,1,0:T(8,128)S(1)} %fusion.12, f32[32]{0:T(128)S(1)} %get-tuple-element.8, s32[32]{0:T(128)S(1)} %bitcast.114), kind=kOutput, calls=%fused_computation.25 | convolution fusion | flops 100925696 | bytes 10486016 | tf_op jit(solution)/shard_map/en,eik->ink/dot_general | solution.py:64
  244.2 0.5 copy_bitcast_fusion
  244.6 2.1 reshape.81
  246.8 0.0 reduce-scatter.5.cloned.1.call-update
  246.8 216.7 %reduce-scatter.5.cloned.1.call-done = f32[8,2048]{1,0:T(8,128)} async-done(((f32[256,2048]{1,0:T(8,128)}), f32[8,2048]{1,0:T(8,128)}) %reduce-scatter.5.cloned.1.call-update) | async-done | bytes 65552
  463.5 0.9 reshape.82
  464.4 24.0 %psum.15 = bf16[8,4,2,256]{3,1,0,2:T(4,128)(2,1)S(1)} all-reduce(f32[8,4,2,256]{3,1,0,2:T(4,128)S(1)} %copy.37), channel_id=1, replica_groups=mesh['src'=8,'snk'=32] {'src'}, use_global_device_ids=true, to_apply=%region_2.3 | all-reduce | flops 16384 | bytes 98304 | tf_op jit(solution)/shard_map/psum | solution.py:73
  488.4 0.7 copy.35
  489.0 0.0 copy-done.1
  (4 shorter events, 0.0 us)
Async XLA Ops:
  6.5 14.3 %copy-start = (f32[16,2]{0,1:T(2,128)S(1)}, f32[16,2]{0,1:T(2,128)}, u32[]{:S(2)}) copy-start(f32[16,2]{0,1:T(2,128)} %param.13) | copy-start | bytes 388
  6.5 23.0 %all-to-all-start = ((bf16[1,32,2,256,8]{3,4,2,0,1:T(8,128)(2,1)}), bf16[1,32,2,256,8]{3,4,2,0,1:T(8,128)(2,1)S(1)}, u32[]{:S(2)}, u32[]{:S(2)}) async-start(bf16[1,32,2,256,8]{3,4,2,0,1:T(8,128)(2,1)} %bitcast.109), calls=%async_computation | async-start | bytes 524288 | tf_op jit(solution)/shard_map/all_to_all | solution.py:36
  18.3 154.5 %all-reduce.2.cloned.1.call-start = ((), (), s32[]{:S(2)}) async-start(), calls=%async_computation.2 | async-start | bytes 2097152 | tf_op jit(solution)/shard_map/psum | solution.py:12
  19.4 444.1 %reduce-scatter.5.cloned.1.call-start = ((), (), s32[]{:S(2)}) async-start(), calls=%async_computation.3 | async-start | bytes 2162688
  179.4 9.1 %copy-start.2 = (bf16[32,2,256,256]{3,2,1,0:T(8,128)(2,1)S(1)}, bf16[32,2,256,256]{3,2,1,0:T(8,128)(2,1)}, u32[]{:S(2)}) copy-start(bf16[32,2,256,256]{3,2,1,0:T(8,128)(2,1)} %gather_fusion) | copy-start | bytes 25165828
  179.4 11.2 %copy-start.3 = (bf16[32,2,256,256]{3,2,1,0:T(8,128)(2,1)S(1)}, bf16[32,2,256,256]{3,2,1,0:T(8,128)(2,1)}, u32[]{:S(2)}) copy-start(bf16[32,2,256,256]{3,2,1,0:T(8,128)(2,1)} %gather_fusion.1) | copy-start | bytes 25165828
  195.2 5.9 %copy-start.4 = (s32[1,1,32]{2,1,0:T(1,128)S(1)}, s32[1,1,32]{2,1,0:T(1,128)}, u32[]{:S(2)}) copy-start(s32[1,1,32]{2,1,0:T(1,128)} %param.11) | copy-start | bytes 388
  225.6 263.4 %copy-start.1 = (f32[16,2]{0,1:T(2,128)S(1)}, f32[16,2]{0,1:T(2,128)}, u32[]{:S(2)}) copy-start(f32[16,2]{0,1:T(2,128)} %param.13) | copy-start | bytes 388
Sparse Core Ops, SparseCore 0:
  22.5 150.1 all-reduce.1
  246.9 216.5 reduce-scatter.4
where the time goes:
time: 499 us; the launch traced here: 496 us
  waiting for transfers between devices  360 us (72%)
  matrix products  64.7 us (13%)
  blocking collectives  24 us (5%)
  local copies, waits for them, and re-layouts  18.8 us (4%)
  between operations  14 us (3%)
  starting transfers between devices  11.8 us (2%)
    unnamed x3, waiting for transfers between devices  217 us
    psum x1, waiting for transfers between devices, from_root(): return lax.psum(kept, axis)  137 us
    psum x1, blocking collectives, shards(): summed = lax.psum(node_share, 'src')  24 us
    all_to_all x1, starting transfers between devices, shards(): lax.all_to_all(peram, 'snk', split_axis=1, concat_axis=4, tiled=True)[0, 0]  11.8 us
  transfers between devices with their start and end apart: 3, of which 3 were waited for; matrix products, arithmetic and copies ran while one was open for 2% of the time, Pallas kernels for 0%

commit v1 on v0

v1 whole, which is shorter than its diff:
```python
import functools

import jax
import jax.numpy as jnp
from jax import lax
from jax.experimental import pallas as pl
from jax.experimental.pallas import tpu as pltpu
from jax.sharding import Mesh, PartitionSpec as P


N = 256
MOM = 4
EDGES = 32
NODES = 4
SNK = 32
ROWS = N // SNK
DEEP = MOM * 2 * N
ALL = ("y", "core", "x", "z")
NY, NC, NX, NZ = 4, 2, 4, 8
BF16 = jnp.bfloat16
F32 = jnp.float32
VMEM_CAP = 14 * 2**20


def mix_kernel(keep, left_e, right_e, node_e, weight_e, table, blocks, mixed, gain):
    core = lax.axis_index("core")
    first = 2 * (core if keep else 1 - core)
    shift = lax.axis_index("x") - lax.axis_index("y") + 2 * NX

    def clear(i, carry):
        gain[0, i] = 0.0
        gain[1, i] = 0.0
        return carry

    lax.fori_loop(0, (NODES + 1) * 16, clear, 0)

    def gather(e, carry):
        key = node_e[0, 0, e] * 16 + right_e[0, 0, e] * 4 + left_e[0, 0, e]
        w = weight_e[0, 0, e]
        gain[0, key] = gain[0, key] + table[0, w]
        gain[1, key] = gain[1, key] + table[1, w]
        return carry

    lax.fori_loop(0, EDGES, gather, 0)
    step = 16

    def rows(r, carry):
        here = pl.ds(pl.multiple_of(r * step, step), step)
        real = [blocks[0, a, 0, here, :].astype(F32) for a in range(MOM)]
        imag = [blocks[0, a, 1, here, :].astype(F32) for a in range(MOM)]
        for n in range(2):
            for d in range(MOM):
                base = (first + n) * 16 + lax.rem(shift - d, MOM) * 4
                wr = [gain[0, base + a] for a in range(MOM)]
                wi = [gain[1, base + a] for a in range(MOM)]
                sum_r = wr[0] * real[0] - wi[0] * imag[0]
                sum_i = wr[0] * imag[0] + wi[0] * real[0]
                for a in range(1, MOM):
                    sum_r = sum_r + (wr[a] * real[a] - wi[a] * imag[a])
                    sum_i = sum_i + (wr[a] * imag[a] + wi[a] * real[a])
                mixed[n, here, (2 * d) * N : (2 * d + 1) * N] = sum_r.astype(BF16)
                mixed[n, here, (2 * d + 1) * N : (2 * d + 2) * N] = sum_i.astype(BF16)
        return carry

    lax.fori_loop(0, N // step, rows, 0)


def mix(keep, left, right, node, weight, table, blocks):
    smem = pl.BlockSpec(memory_space=pltpu.SMEM)
    vmem = pl.BlockSpec(memory_space=pltpu.VMEM)
    return pl.pallas_call(
        functools.partial(mix_kernel, keep),
        out_shape=jax.ShapeDtypeStruct((2, N, DEEP), BF16),
        in_specs=[smem] * 5 + [vmem],
        out_specs=vmem,
        scratch_shapes=[pltpu.SMEM((2, 128), F32)],
        cost_estimate=pl.CostEstimate(
            flops=2 * MOM * MOM * 8 * N * N,
            bytes_accessed=(MOM * 2 + 2 * MOM * 2) * N * N * 2,
            transcendentals=0,
        ),
        name="mix_keep" if keep else "mix_send",
    )(left, right, node, weight, table, blocks)


def half_product(mixed, stack, out):
    parts = [
        jnp.dot(mixed[n], stack[...], preferred_element_type=F32).reshape(SNK, ROWS, 2 * N)
        for n in range(2)
    ]
    out[...] = jnp.concatenate(parts, 1).astype(out.dtype)


def send_kernel(tau_t, r0, r1, r2, r3, mixed, send, stack):
    tau = [
        tau_t[:, p].astype(F32).reshape(N, N).T.astype(BF16) for p in range(2)
    ]
    for d, block in enumerate((r0, r1, r2, r3)):
        real = jnp.dot(tau[0], block[0], preferred_element_type=F32) - jnp.dot(
            tau[1], block[1], preferred_element_type=F32
        )
        imag = jnp.dot(tau[0], block[1], preferred_element_type=F32) + jnp.dot(
            tau[1], block[0], preferred_element_type=F32
        )
        top, low = 2 * d * N, (2 * d + 1) * N
        stack[top : top + N, :N] = real.astype(BF16)
        stack[top : top + N, N:] = imag.astype(BF16)
        stack[low : low + N, :N] = (-imag).astype(BF16)
        stack[low : low + N, N:] = real.astype(BF16)
    half_product(mixed, stack, send)


def send_half(tau_t, right, mixed):
    vmem = pl.BlockSpec(memory_space=pltpu.VMEM)
    return pl.pallas_call(
        send_kernel,
        out_shape=(
            jax.ShapeDtypeStruct((SNK, 2 * ROWS, 2 * N), BF16),
            jax.ShapeDtypeStruct((DEEP, 2 * N), BF16),
        ),
        in_specs=[vmem] * 6,
        out_specs=(vmem, vmem),
        compiler_params=pltpu.CompilerParams(vmem_limit_bytes=VMEM_CAP),
        cost_estimate=pl.CostEstimate(
            flops=2 * (MOM * 4 + 2 * MOM * 4) * N * N * N,
            bytes_accessed=6 * 2**20,
            transcendentals=0,
        ),
        name="send_half",
    )(tau_t, *right, mixed)


def keep_half(mixed, stack):
    vmem = pl.BlockSpec(memory_space=pltpu.VMEM)
    return pl.pallas_call(
        half_product,
        out_shape=jax.ShapeDtypeStruct((SNK, 2 * ROWS, 2 * N), F32),
        in_specs=[vmem] * 2,
        out_specs=vmem,
        compiler_params=pltpu.CompilerParams(vmem_limit_bytes=VMEM_CAP),
        cost_estimate=pl.CostEstimate(
            flops=2 * 2 * MOM * 4 * N * N * N,
            bytes_accessed=5 * 2**20,
            transcendentals=0,
        ),
        name="keep_half",
    )(mixed, stack)


def device(y, c, x, z):
    return ((y * NC + c) * NX + x % NX) * NZ + z % NZ


def spread(block):
    x, z = lax.axis_index("x"), lax.axis_index("z")
    y, c = lax.axis_index("y"), lax.axis_index("core")
    lines = [(a, b, i) for a in range(NY) for b in range(NC) for i in range(NX)]

    def along_z(value, hops):
        pairs = [
            (device(a, b, i, 4 * b + u), device(a, b, i, 4 * b + v))
            for a, b, i in lines
            for u, v in hops
        ]
        return lax.ppermute(value, ALL, pairs)

    def home(value, k):
        pairs = [
            (device(b, c, a, j), device(a, c, b + k, j))
            for a in range(NX)
            for b in range(NY)
            for c in range(NC)
            for j in range(NZ)
        ]
        return lax.ppermute(value, ALL, pairs)

    where_z = lax.rem(z - 4 * c + NZ, NZ)
    own = lax.dynamic_index_in_dim(block, lax.rem(y - x + NX, NX), 0, keepdims=False)
    got = []
    for d in (4, 3, 5, 2, 6, 1, 7):
        got.append(along_z(own, [(0, d)]))
    part = jnp.where(where_z == 0, own, functools.reduce(jnp.add, got))
    pieces = []
    for k in range(NX):
        pieces.append(home(part, k))
    return pieces


def shards(peram, meson_blocks, edge_left, edge_right, edge_node, edge_weight, weight_table):
    return contract(
        peram,
        meson_blocks,
        (edge_left, edge_right, edge_node, edge_weight, weight_table.T),
    )


def contract(peram, meson_blocks, edges):
    core = lax.axis_index("core")
    by_time = jnp.swapaxes(peram[0], 2, 3)
    tau_t = lax.all_to_all(by_time, ("x", "z"), split_axis=0, concat_axis=0, tiled=True)
    mixed_send = mix(False, *edges, meson_blocks)
    mixed_keep = mix(True, *edges, meson_blocks)
    right = spread(meson_blocks[0])
    send, stack = send_half(tau_t, right, mixed_send)
    got = lax.ppermute(send, "core", [(0, 1), (1, 0)])
    keep = keep_half(mixed_keep, stack)
    pair = (keep + got.astype(F32)).astype(BF16)
    times = lax.all_to_all(pair, ("x", "z"), split_axis=0, concat_axis=0, tiled=True)
    one = jnp.sum(times.astype(F32), 0)
    total = one
    for d in range(1, NY):
        total = total + lax.ppermute(one, "y", [(i, (i + d) % NY) for i in range(NY)])
    mine = total.astype(BF16)
    other = lax.ppermute(mine, "core", [(0, 1), (1, 0)])
    halves = jnp.where(core == 0, jnp.stack([mine, other]), jnp.stack([other, mine]))
    halves = halves.reshape(2, 2, ROWS, 2, N)
    return jnp.transpose(halves, (2, 0, 1, 3, 4)).reshape(ROWS, NODES, 2, N)


def solution(mesh):
    fine = Mesh(mesh.devices.reshape(NY, NC, NX, NZ), ALL)
    src, snk = ("y", "core"), ("x", "z")
    edges = P(src, snk, None)
    return jax.shard_map(
        shards,
        mesh=fine,
        in_specs=(
            P(src, None, None, None, snk),
            P(snk, None, None, None, None),
            edges,
            edges,
            edges,
            edges,
            P(),
        ),
        out_specs=P(snk, None, None, None),
        check_vma=False,
    )
```

time: 499 us -> 102 us (0.20)
  the two profiles are of different devices: /device:TPU:2 before, /device:TPU:1 now
where the time goes in v1:
time: 102 us
  starting transfers between devices  38.3 us (38%)
  blocking collectives  27.7 us (27%)
  Pallas kernels  15.1 us (15%)
  waiting for transfers between devices  11.1 us (11%)
  local copies, waits for them, and re-layouts  8.12 us (8%)
  other arithmetic  1.37 us (1%)
    all_to_all x1, blocking collectives, contract(): lax.all_to_all(pair, ('x', 'z'), split_axis=0, concat_axis=0, tiled=True)  27.7 us
    all_to_all x1, starting transfers between devices, contract(): lax.all_to_all(by_time, ('x', 'z'), split_axis=0, concat_axis=0, tiled=True)  16.4 us
    pallas_call x2, Pallas kernels, mix(): pl.pallas_call(functools.partial(mix_kernel, keep), out_shape=jax.ShapeDt...  12.1 us
    ppermute x4, starting transfers between devices, home(): return lax.ppermute(value, ALL, pairs)  7.04 us
    unnamed x12, local copies, waits for them, and re-layouts  6.49 us
    ppermute x7, starting transfers between devices, along_z(): return lax.ppermute(value, ALL, pairs)  5.36 us
    ppermute x4, waiting for transfers between devices, home(): return lax.ppermute(value, ALL, pairs)  4.9 us
    ppermute x1, starting transfers between devices, contract(): other = lax.ppermute(mine, 'core', [(0, 1), (1, 0)])  4.55 us
  transfers between devices with their start and end apart: 17, of which 6 were waited for; matrix products, arithmetic and copies ran while one was open for 1% of the time, Pallas kernels for 13%

profile of v1, /device:TPU:1, one launch (start us, length us, event | category | flops | bytes accessed | tf_op | source)
XLA Modules:
  0.0 101.9 jit_solution(5311637594269474301)
XLA Ops:
  0.0 1.0 dynamic-slice_bitcast_fusion
  1.0 0.7 collective-permute-start.6
  1.7 0.7 collective-permute-start.5
  2.3 0.7 collective-permute-start.4
  3.0 0.7 collective-permute-start.3
  3.7 0.7 collective-permute-start.2
  4.4 0.0 collective-permute-done.6
  4.4 0.7 collective-permute-start.1
  5.1 0.0 collective-permute-done.5
  5.1 1.3 %collective-permute-start = (bf16[2,256,256]{2,1,0:T(8,128)(2,1)S(1)}, bf16[2,256,256]{2,1,0:T(8,128)(2,1)S(1)}, u32[]{:S(2)}, u32[]{:S(2)}) collective-permute-start(bf16[2,256,256]{2,1,0:T(8,128)(2,1)S(1)} %dynamic-slice_bitcast_fusion), channel_id=1, source_target_pairs={{0,4},{8,12},{16,20},{24,28},{36,32},{44,40},{52,48},{60,56},{64,6... | collective-permute-start | bytes 786440 | tf_op jit(solution)/shard_map/ppermute | solution.py:165
  6.4 16.4 %all-to-all-start = ((bf16[32,2,8,256]{3,2,1,0:T(8,128)(2,1)}), bf16[32,2,8,256]{3,2,1,0:T(8,128)(2,1)S(1)}, u32[]{:S(2)}, u32[]{:S(2)}) async-start(bf16[32,2,8,256]{3,2,1,0:T(8,128)(2,1)} %bitcast.11), calls=%async_computation | async-start | bytes 524288 | tf_op jit(solution)/shard_map/all_to_all | solution.py:200
  22.8 0.0 collective-permute-done.4
  22.8 0.0 collective-permute-done.3
  22.8 0.0 collective-permute-done.2
  22.8 0.0 collective-permute-done.1
  22.8 1.4 %collective-permute-done = bf16[2,256,256]{2,1,0:T(8,128)(2,1)S(1)} collective-permute-done((bf16[2,256,256]{2,1,0:T(8,128)(2,1)S(1)}, bf16[2,256,256]{2,1,0:T(8,128)(2,1)S(1)}, u32[]{:S(2)}, u32[]{:S(2)}) %collective-permute-start) | collective-permute-done | bytes 262176 | tf_op jit(solution)/shard_map/ppermute | solution.py:165
  24.2 1.0 %add_select_fusion = bf16[2,256,256]{2,1,0:T(8,128)(2,1)S(1)} fusion(bf16[2,256,256]{2,1,0:T(8,128)(2,1)S(1)} %collective-permute-done.6, bf16[2,256,256]{2,1,0:T(8,128)(2,1)S(1)} %collective-permute-done.5, bf16[2,256,256]{2,1,0:T(8,128)(2,1)S(1)} %collective-permute-done.4, bf16[2,256,256]{2,1,0:T(8,128)(2,1)S(1)} %collective-permute-done.3, ...), kind=kLoop, calls=%fused_computation.2 | loop fusion | flops 917504 | bytes 2359301 | tf_op jit(solution)/shard_map/jit(_where)/select_n | solution.py:182
  25.2 2.6 %collective-permute-start.10 = (bf16[2,256,256]{2,1,0:T(8,128)(2,1)S(1)}, bf16[2,256,256]{2,1,0:T(8,128)(2,1)S(1)}, u32[]{:S(2)}, u32[]{:S(2)}) collective-permute-start(bf16[2,256,256]{2,1,0:T(8,128)(2,1)S(1)} %add_select_fusion), channel_id=1, source_target_pairs={{0,24},{1,25},{2,26},{3,27},{4,28},{5,29},{6,30},{7,31},{32,56},{3... | collective-permute-start | bytes 786440 | tf_op jit(solution)/shard_map/ppermute | solution.py:175
  27.8 3.8 %collective-permute-start.9 = (bf16[2,256,256]{2,1,0:T(8,128)(2,1)S(1)}, bf16[2,256,256]{2,1,0:T(8,128)(2,1)S(1)}, u32[]{:S(2)}, u32[]{:S(2)}) collective-permute-start(bf16[2,256,256]{2,1,0:T(8,128)(2,1)S(1)} %add_select_fusion), channel_id=1, source_target_pairs={{0,16},{1,17},{2,18},{3,19},{4,20},{5,21},{6,22},{7,23},{32,48},{3... | collective-permute-start | bytes 786440 | tf_op jit(solution)/shard_map/ppermute | solution.py:175
  31.6 0.0 collective-permute-start.8
  31.6 0.7 collective-permute-start.7
  32.3 6.0 %mix_send.1.mixed = bf16[2,256,2048]{2,1,0:T(8,128)(2,1)} custom-call(s32[1,1,32]{2,1,0:T(1,128)} %left_e.3, s32[1,1,32]{2,1,0:T(1,128)} %right_e.3, s32[1,1,32]{2,1,0:T(1,128)} %node_e.3, s32[1,1,32]{2,1,0:T(1,128)} %weight_e.3, f32[2,16]{1,0:T(2,128)} %bitcast.13, bf16[1,4,2,256,256]{4,3,2,1,0:T(8,128)(2,1)} %blocks.3), custom_call_target="tpu_custom_call" | custom-call | flops 16777216 | bytes 3145728 | tf_op jit(solution)/shard_map/mix_send/pallas_call | solution.py:71
  38.3 0.0 all-to-all-done.tau_t
  38.3 2.8 %collective-permute-done.10.r3 = bf16[2,256,256]{2,1,0:T(8,128)(2,1)S(1)} collective-permute-done((bf16[2,256,256]{2,1,0:T(8,128)(2,1)S(1)}, bf16[2,256,256]{2,1,0:T(8,128)(2,1)S(1)}, u32[]{:S(2)}, u32[]{:S(2)}) %collective-permute-start.10) | collective-permute-done | bytes 262176 | tf_op jit(solution)/shard_map/ppermute | solution.py:175
  41.2 0.0 collective-permute-done.9.r2
  41.2 2.1 %collective-permute-done.8.r1 = bf16[2,256,256]{2,1,0:T(8,128)(2,1)S(1)} collective-permute-done((bf16[2,256,256]{2,1,0:T(8,128)(2,1)S(1)}, bf16[2,256,256]{2,1,0:T(8,128)(2,1)S(1)}, u32[]{:S(2)}, u32[]{:S(2)}) %collective-permute-start.8) | collective-permute-done | bytes 262176 | tf_op jit(solution)/shard_map/ppermute | solution.py:175
  43.2 0.0 copy-start.2
  43.2 0.7 copy-done.2
  43.9 0.0 collective-permute-done.7.r0
  43.9 0.0 copy-start.4
  43.9 0.7 copy-done.4
  44.7 0.0 copy-start.1
  44.7 1.6 %copy-done.1 = bf16[2,256,2048]{2,1,0:T(8,128)(2,1)S(1)} copy-done((bf16[2,256,2048]{2,1,0:T(8,128)(2,1)S(1)}, bf16[2,256,2048]{2,1,0:T(8,128)(2,1)}, u32[]{:S(2)}) %copy-start.1) | copy-done | bytes 2097176
  46.2 0.0 copy-start.3
  46.2 0.9 copy-done.3
  47.2 0.0 copy-start.5
  47.2 0.9 copy-done.5
  48.1 1.8 %send_half.1 = (bf16[32,16,512]{2,1,0:T(8,128)(2,1)S(1)}, bf16[2048,512]{1,0:T(8,128)(2,1)S(1)}) custom-call(bf16[32,2,8,256]{3,2,1,0:T(8,128)(2,1)S(1)} %all-to-all-done.tau_t, bf16[2,256,256]{2,1,0:T(8,128)(2,1)S(1)} %copy-done.5, bf16[2,256,256]{2,1,0:T(8,128)(2,1)S(1)} %copy-done.3, bf16[2,256,256]{2,1,0:T(8,128)(2,1)S(1)} %collective-permute-done.9.r2, ...), custom_call_target="tpu_custom_call" | custom-call | flops 1610612736 | bytes 6291456 | tf_op jit(solution)/shard_map/send_half/pallas_call | solution.py:115
  50.0 0.6 collective-permute-start.11
  50.6 6.0 %mix_keep.1.mixed = bf16[2,256,2048]{2,1,0:T(8,128)(2,1)} custom-call(s32[1,1,32]{2,1,0:T(1,128)} %left_e.3, s32[1,1,32]{2,1,0:T(1,128)} %right_e.3, s32[1,1,32]{2,1,0:T(1,128)} %node_e.3, s32[1,1,32]{2,1,0:T(1,128)} %weight_e.3, f32[2,16]{1,0:T(2,128)} %bitcast.14, bf16[1,4,2,256,256]{4,3,2,1,0:T(8,128)(2,1)} %blocks.3), custom_call_target="tpu_custom_call" | custom-call | flops 16777216 | bytes 3145728 | tf_op jit(solution)/shard_map/mix_keep/pallas_call | solution.py:71
  56.6 0.0 copy-start
  56.6 1.6 %copy-done = bf16[2,256,2048]{2,1,0:T(8,128)(2,1)S(1)} copy-done((bf16[2,256,2048]{2,1,0:T(8,128)(2,1)S(1)}, bf16[2,256,2048]{2,1,0:T(8,128)(2,1)}, u32[]{:S(2)}) %copy-start) | copy-done | bytes 2097176
  58.2 1.2 %keep_half.1 = f32[32,16,512]{2,1,0:T(8,128)S(1)} custom-call(bf16[2,256,2048]{2,1,0:T(8,128)(2,1)S(1)} %copy-done, bf16[2048,512]{1,0:T(8,128)(2,1)S(1)} %get-tuple-element.7.stack), custom_call_target="tpu_custom_call" | custom-call | flops 1073741824 | bytes 5242880 | tf_op jit(solution)/shard_map/keep_half/pallas_call | solution.py:135
  59.5 0.0 collective-permute-done.11
  59.5 0.2 add_convert_fusion
  59.7 27.7 %all_to_all.10 = bf16[32,16,512]{2,1,0:T(8,128)(2,1)S(1)} all-to-all(bf16[32,16,512]{2,1,0:T(8,128)(2,1)S(1)} %add_convert_fusion), channel_id=1, replica_groups=mesh['y'=4,'core'=2,'x'=4,'z'=8] {'x','z'}, dimensions={0} | all-to-all | bytes 1048576 | tf_op jit(solution)/shard_map/all_to_all | solution.py:208
  87.3 0.1 convert_reduce_fusion
  87.4 3.1 %collective-permute-start.14 = (f32[16,512]{1,0:T(8,128)S(1)}, f32[16,512]{1,0:T(8,128)S(1)}, u32[]{:S(2)}, u32[]{:S(2)}) collective-permute-start(f32[16,512]{1,0:T(8,128)S(1)} %convert_reduce_fusion), channel_id=1, source_target_pairs={{0,192},{64,0},{128,64},{192,128},{1,193},{65,1},{129,65},{193,129... | collective-permute-start | bytes 98312 | tf_op jit(solution)/shard_map/ppermute | solution.py:212
  90.6 1.2 %collective-permute-start.13 = (f32[16,512]{1,0:T(8,128)S(1)}, f32[16,512]{1,0:T(8,128)S(1)}, u32[]{:S(2)}, u32[]{:S(2)}) collective-permute-start(f32[16,512]{1,0:T(8,128)S(1)} %convert_reduce_fusion), channel_id=1, source_target_pairs={{0,128},{64,192},{128,0},{192,64},{1,129},{65,193},{129,1},{193,65... | collective-permute-start | bytes 98312 | tf_op jit(solution)/shard_map/ppermute | solution.py:212
  91.8 0.0 collective-permute-start.12
  91.8 0.0 collective-permute-done.14
  91.8 3.1 %collective-permute-done.13 = f32[16,512]{1,0:T(8,128)S(1)} collective-permute-done((f32[16,512]{1,0:T(8,128)S(1)}, f32[16,512]{1,0:T(8,128)S(1)}, u32[]{:S(2)}, u32[]{:S(2)}) %collective-permute-start.13) | collective-permute-done | bytes 32800 | tf_op jit(solution)/shard_map/ppermute | solution.py:212
  94.8 0.9 collective-permute-done.12
  95.8 4.5 %collective-permute-start.15 = (bf16[16,512]{1,0:T(8,128)(2,1)S(1)}, bf16[16,512]{1,0:T(8,128)(2,1)S(1)}, u32[]{:S(2)}, u32[]{:S(2)}) collective-permute-start(bf16[16,512]{1,0:T(8,128)(2,1)S(1)} %add_convert_fusion.1), channel_id=1, source_target_pairs={{0,32},{32,0},{1,33},{33,1},{2,34},{34,2},{3,35},{35,3},{4,36},{36... | collective-permute-start | bytes 49160 | tf_op jit(solution)/shard_map/ppermute | solution.py:214
  100.3 0.8 collective-permute-done.15
  101.2 0.1 broadcast_select_fusion
  101.2 0.6 copy.8
  (3 shorter events, 0.0 us)
Async XLA Ops:
  1.0 3.4 %collective-permute-start.6 = (bf16[2,256,256]{2,1,0:T(8,128)(2,1)S(1)}, bf16[2,256,256]{2,1,0:T(8,128)(2,1)S(1)}, u32[]{:S(2)}, u32[]{:S(2)}) collective-permute-start(bf16[2,256,256]{2,1,0:T(8,128)(2,1)S(1)} %dynamic-slice_bitcast_fusion), channel_id=1, source_target_pairs={{0,7},{8,15},{16,23},{24,31},{36,35},{44,43},{52,51},{60,59},{64,7... | collective-permute-start | bytes 786440 | tf_op jit(solution)/shard_map/ppermute | solution.py:165
  1.7 3.4 %collective-permute-start.5 = (bf16[2,256,256]{2,1,0:T(8,128)(2,1)S(1)}, bf16[2,256,256]{2,1,0:T(8,128)(2,1)S(1)}, u32[]{:S(2)}, u32[]{:S(2)}) collective-permute-start(bf16[2,256,256]{2,1,0:T(8,128)(2,1)S(1)} %dynamic-slice_bitcast_fusion), channel_id=1, source_target_pairs={{0,1},{8,9},{16,17},{24,25},{36,37},{44,45},{52,53},{60,61},{64,65... | collective-permute-start | bytes 786440 | tf_op jit(solution)/shard_map/ppermute | solution.py:165
  2.3 20.5 %collective-permute-start.4 = (bf16[2,256,256]{2,1,0:T(8,128)(2,1)S(1)}, bf16[2,256,256]{2,1,0:T(8,128)(2,1)S(1)}, u32[]{:S(2)}, u32[]{:S(2)}) collective-permute-start(bf16[2,256,256]{2,1,0:T(8,128)(2,1)S(1)} %dynamic-slice_bitcast_fusion), channel_id=1, source_target_pairs={{0,6},{8,14},{16,22},{24,30},{36,34},{44,42},{52,50},{60,58},{64,7... | collective-permute-start | bytes 786440 | tf_op jit(solution)/shard_map/ppermute | solution.py:165
  3.0 19.8 %collective-permute-start.3 = (bf16[2,256,256]{2,1,0:T(8,128)(2,1)S(1)}, bf16[2,256,256]{2,1,0:T(8,128)(2,1)S(1)}, u32[]{:S(2)}, u32[]{:S(2)}) collective-permute-start(bf16[2,256,256]{2,1,0:T(8,128)(2,1)S(1)} %dynamic-slice_bitcast_fusion), channel_id=1, source_target_pairs={{0,2},{8,10},{16,18},{24,26},{36,38},{44,46},{52,54},{60,62},{64,6... | collective-permute-start | bytes 786440 | tf_op jit(solution)/shard_map/ppermute | solution.py:165
  3.7 19.1 %collective-permute-start.2 = (bf16[2,256,256]{2,1,0:T(8,128)(2,1)S(1)}, bf16[2,256,256]{2,1,0:T(8,128)(2,1)S(1)}, u32[]{:S(2)}, u32[]{:S(2)}) collective-permute-start(bf16[2,256,256]{2,1,0:T(8,128)(2,1)S(1)} %dynamic-slice_bitcast_fusion), channel_id=1, source_target_pairs={{0,5},{8,13},{16,21},{24,29},{36,33},{44,41},{52,49},{60,57},{64,6... | collective-permute-start | bytes 786440 | tf_op jit(solution)/shard_map/ppermute | solution.py:165
  4.4 18.4 %collective-permute-start.1 = (bf16[2,256,256]{2,1,0:T(8,128)(2,1)S(1)}, bf16[2,256,256]{2,1,0:T(8,128)(2,1)S(1)}, u32[]{:S(2)}, u32[]{:S(2)}) collective-permute-start(bf16[2,256,256]{2,1,0:T(8,128)(2,1)S(1)} %dynamic-slice_bitcast_fusion), channel_id=1, source_target_pairs={{0,3},{8,11},{16,19},{24,27},{36,39},{44,47},{52,55},{60,63},{64,6... | collective-permute-start | bytes 786440 | tf_op jit(solution)/shard_map/ppermute | solution.py:165
  5.1 19.1 %collective-permute-start = (bf16[2,256,256]{2,1,0:T(8,128)(2,1)S(1)}, bf16[2,256,256]{2,1,0:T(8,128)(2,1)S(1)}, u32[]{:S(2)}, u32[]{:S(2)}) collective-permute-start(bf16[2,256,256]{2,1,0:T(8,128)(2,1)S(1)} %dynamic-slice_bitcast_fusion), channel_id=1, source_target_pairs={{0,4},{8,12},{16,20},{24,28},{36,32},{44,40},{52,48},{60,56},{64,6... | collective-permute-start | bytes 786440 | tf_op jit(solution)/shard_map/ppermute | solution.py:165
  6.4 31.9 %all-to-all-start = ((bf16[32,2,8,256]{3,2,1,0:T(8,128)(2,1)}), bf16[32,2,8,256]{3,2,1,0:T(8,128)(2,1)S(1)}, u32[]{:S(2)}, u32[]{:S(2)}) async-start(bf16[32,2,8,256]{3,2,1,0:T(8,128)(2,1)} %bitcast.11), calls=%async_computation | async-start | bytes 524288 | tf_op jit(solution)/shard_map/all_to_all | solution.py:200
  25.2 15.9 %collective-permute-start.10 = (bf16[2,256,256]{2,1,0:T(8,128)(2,1)S(1)}, bf16[2,256,256]{2,1,0:T(8,128)(2,1)S(1)}, u32[]{:S(2)}, u32[]{:S(2)}) collective-permute-start(bf16[2,256,256]{2,1,0:T(8,128)(2,1)S(1)} %add_select_fusion), channel_id=1, source_target_pairs={{0,24},{1,25},{2,26},{3,27},{4,28},{5,29},{6,30},{7,31},{32,56},{3... | collective-permute-start | bytes 786440 | tf_op jit(solution)/shard_map/ppermute | solution.py:175
  27.8 13.4 %collective-permute-start.9 = (bf16[2,256,256]{2,1,0:T(8,128)(2,1)S(1)}, bf16[2,256,256]{2,1,0:T(8,128)(2,1)S(1)}, u32[]{:S(2)}, u32[]{:S(2)}) collective-permute-start(bf16[2,256,256]{2,1,0:T(8,128)(2,1)S(1)} %add_select_fusion), channel_id=1, source_target_pairs={{0,16},{1,17},{2,18},{3,19},{4,20},{5,21},{6,22},{7,23},{32,48},{3... | collective-permute-start | bytes 786440 | tf_op jit(solution)/shard_map/ppermute | solution.py:175
  31.6 11.6 %collective-permute-start.8 = (bf16[2,256,256]{2,1,0:T(8,128)(2,1)S(1)}, bf16[2,256,256]{2,1,0:T(8,128)(2,1)S(1)}, u32[]{:S(2)}, u32[]{:S(2)}) collective-permute-start(bf16[2,256,256]{2,1,0:T(8,128)(2,1)S(1)} %add_select_fusion), channel_id=1, source_target_pairs={{0,8},{1,9},{2,10},{3,11},{4,12},{5,13},{6,14},{7,15},{32,40},{33,... | collective-permute-start | bytes 786440 | tf_op jit(solution)/shard_map/ppermute | solution.py:175
  31.6 12.3 %collective-permute-start.7 = (bf16[2,256,256]{2,1,0:T(8,128)(2,1)S(1)}, bf16[2,256,256]{2,1,0:T(8,128)(2,1)S(1)}, u32[]{:S(2)}, u32[]{:S(2)}) collective-permute-start(bf16[2,256,256]{2,1,0:T(8,128)(2,1)S(1)} %add_select_fusion), channel_id=1, source_target_pairs={{0,0},{1,1},{2,2},{3,3},{4,4},{5,5},{6,6},{7,7},{32,32},{33,33},{3... | collective-permute-start | bytes 786440 | tf_op jit(solution)/shard_map/ppermute | solution.py:175
  43.2 0.7 copy-start.2
  43.9 0.7 copy-start.4
  44.7 1.6 %copy-start.1 = (bf16[2,256,2048]{2,1,0:T(8,128)(2,1)S(1)}, bf16[2,256,2048]{2,1,0:T(8,128)(2,1)}, u32[]{:S(2)}) copy-start(bf16[2,256,2048]{2,1,0:T(8,128)(2,1)} %mix_send.1.mixed) | copy-start | bytes 6291460
  46.2 0.9 copy-start.3
  47.2 0.9 copy-start.5
  50.0 9.5 %collective-permute-start.11 = (bf16[32,16,512]{2,1,0:T(8,128)(2,1)S(1)}, bf16[32,16,512]{2,1,0:T(8,128)(2,1)S(1)}, u32[]{:S(2)}, u32[]{:S(2)}) collective-permute-start(bf16[32,16,512]{2,1,0:T(8,128)(2,1)S(1)} %get-tuple-element.8), channel_id=1, source_target_pairs={{0,32},{32,0},{1,33},{33,1},{2,34},{34,2},{3,35},{35,3},{4,36},{36... | collective-permute-start | bytes 1572872 | tf_op jit(solution)/shard_map/ppermute | solution.py:205
  56.6 1.6 %copy-start = (bf16[2,256,2048]{2,1,0:T(8,128)(2,1)S(1)}, bf16[2,256,2048]{2,1,0:T(8,128)(2,1)}, u32[]{:S(2)}) copy-start(bf16[2,256,2048]{2,1,0:T(8,128)(2,1)} %mix_keep.1.mixed) | copy-start | bytes 6291460
  87.4 4.4 %collective-permute-start.14 = (f32[16,512]{1,0:T(8,128)S(1)}, f32[16,512]{1,0:T(8,128)S(1)}, u32[]{:S(2)}, u32[]{:S(2)}) collective-permute-start(f32[16,512]{1,0:T(8,128)S(1)} %convert_reduce_fusion), channel_id=1, source_target_pairs={{0,192},{64,0},{128,64},{192,128},{1,193},{65,1},{129,65},{193,129... | collective-permute-start | bytes 98312 | tf_op jit(solution)/shard_map/ppermute | solution.py:212
  90.6 4.3 %collective-permute-start.13 = (f32[16,512]{1,0:T(8,128)S(1)}, f32[16,512]{1,0:T(8,128)S(1)}, u32[]{:S(2)}, u32[]{:S(2)}) collective-permute-start(f32[16,512]{1,0:T(8,128)S(1)} %convert_reduce_fusion), channel_id=1, source_target_pairs={{0,128},{64,192},{128,0},{192,64},{1,129},{65,193},{129,1},{193,65... | collective-permute-start | bytes 98312 | tf_op jit(solution)/shard_map/ppermute | solution.py:212
  91.8 4.0 %collective-permute-start.12 = (f32[16,512]{1,0:T(8,128)S(1)}, f32[16,512]{1,0:T(8,128)S(1)}, u32[]{:S(2)}, u32[]{:S(2)}) collective-permute-start(f32[16,512]{1,0:T(8,128)S(1)} %convert_reduce_fusion), channel_id=1, source_target_pairs={{0,64},{64,128},{128,192},{192,0},{1,65},{65,129},{129,193},{193,1... | collective-permute-start | bytes 98312 | tf_op jit(solution)/shard_map/ppermute | solution.py:212
  95.8 5.4 %collective-permute-start.15 = (bf16[16,512]{1,0:T(8,128)(2,1)S(1)}, bf16[16,512]{1,0:T(8,128)(2,1)S(1)}, u32[]{:S(2)}, u32[]{:S(2)}) collective-permute-start(bf16[16,512]{1,0:T(8,128)(2,1)S(1)} %add_convert_fusion.1), channel_id=1, source_target_pairs={{0,32},{32,0},{1,33},{33,1},{2,34},{34,2},{3,35},{35,3},{4,36},{36... | collective-permute-start | bytes 49160 | tf_op jit(solution)/shard_map/ppermute | solution.py:214

commit v2 on v1

v2 whole, which is shorter than its diff:
```python
import functools

import jax
import jax.numpy as jnp
from jax import lax
from jax.experimental import pallas as pl
from jax.experimental.pallas import tpu as pltpu
from jax.sharding import Mesh, PartitionSpec as P


N = 256
MOM = 4
EDGES = 32
NODES = 4
SNK = 32
ROWS = N // SNK
DEEP = MOM * 2 * N
ALL = ("y", "core", "x", "z")
NY, NC, NX, NZ = 4, 2, 4, 8
BF16 = jnp.bfloat16
F32 = jnp.float32
VMEM_CAP = 48 * 2**20
CHUNK = 64
POSTS = (0, 3)
LINES = ((6, 5), (7, 2), (1, 4))
MIX_CAP = 60 * 2**20
ROUND = (2, 1, 3)


def mix_kernel(left_e, right_e, node_e, weight_e, table, blocks, out, gain):
    core = lax.axis_index("core")
    shift = lax.axis_index("x") - lax.axis_index("y") + 2 * NX

    @pl.when(pl.program_id(0) == 0)
    def fold_edges():
        def clear(i, carry):
            gain[0, i] = 0.0
            gain[1, i] = 0.0
            return carry

        lax.fori_loop(0, (NODES + 1) * 16, clear, 0)

        def gather(e, carry):
            key = node_e[0, 0, e] * 16 + right_e[0, 0, e] * 4 + left_e[0, 0, e]
            w = weight_e[0, 0, e]
            gain[0, key] = gain[0, key] + table[0, w]
            gain[1, key] = gain[1, key] + table[1, w]
            return carry

        lax.fori_loop(0, EDGES, gather, 0)

    step = 16

    def rows(r, carry):
        here = pl.ds(pl.multiple_of(r * step, step), step)
        real = [blocks[0, a, 0, here, :].astype(F32) for a in range(MOM)]
        imag = [blocks[0, a, 1, here, :].astype(F32) for a in range(MOM)]
        both = [u + v for u, v in zip(real, imag)]
        for n in range(NODES):
            for d in range(MOM):
                base = lax.rem(n + 2 - 2 * core, NODES) * 16 + lax.rem(shift - d, MOM) * 4
                wr = [gain[0, base + a] for a in range(MOM)]
                wi = [gain[1, base + a] for a in range(MOM)]
                mid = sum(wr[a] * both[a] for a in range(1, MOM)) + wr[0] * both[0]
                low = sum((wr[a] + wi[a]) * imag[a] for a in range(1, MOM))
                low = low + (wr[0] + wi[0]) * imag[0]
                top = sum((wi[a] - wr[a]) * real[a] for a in range(1, MOM))
                top = top + (wi[0] - wr[0]) * real[0]
                out[n, here, (2 * d) * N : (2 * d + 1) * N] = (mid - low).astype(BF16)
                out[n, here, (2 * d + 1) * N : (2 * d + 2) * N] = (mid + top).astype(BF16)
        return carry

    lax.fori_loop(0, CHUNK // step, rows, 0)


def mix(left, right, node, weight, table, blocks):
    smem = pl.BlockSpec(memory_space=pltpu.SMEM)
    half = pl.BlockSpec((NODES, CHUNK, DEEP), lambda i: (0, i, 0))
    return pl.pallas_call(
        mix_kernel,
        grid=(N // CHUNK,),
        out_shape=jax.ShapeDtypeStruct((NODES, N, DEEP), BF16),
        in_specs=[smem] * 5 + [pl.BlockSpec((1, MOM, 2, CHUNK, N), lambda i: (0, 0, 0, i, 0))],
        out_specs=half,
        scratch_shapes=[pltpu.SMEM((2, 128), F32)],
        compiler_params=pltpu.CompilerParams(vmem_limit_bytes=MIX_CAP),
        cost_estimate=pl.CostEstimate(
            flops=4 * MOM * MOM * 8 * N * N,
            bytes_accessed=(MOM * 2 + 4 * MOM * 2) * N * N * 2,
            transcendentals=0,
        ),
        name="mix",
    )(left, right, node, weight, table, blocks)


def half_product(mixed, stack, out):
    parts = [
        jnp.dot(mixed[n], stack[...], preferred_element_type=F32).reshape(SNK, ROWS, 2 * N)
        for n in range(2)
    ]
    out[...] = jnp.concatenate(parts, 1).astype(out.dtype)


def send_kernel(tau_t, r0, r1, r2, r3, mixed_any, send, stack, mixed, arrived):
    fetch = pltpu.make_async_copy(mixed_any.at[0:2], mixed, arrived)
    fetch.start()
    tau = [
        tau_t[:, p].astype(F32).reshape(N, N).T.astype(BF16) for p in range(2)
    ]
    for d, block in enumerate((r0, r1, r2, r3)):
        real = jnp.dot(tau[0], block[0], preferred_element_type=F32) - jnp.dot(
            tau[1], block[1], preferred_element_type=F32
        )
        imag = jnp.dot(tau[0], block[1], preferred_element_type=F32) + jnp.dot(
            tau[1], block[0], preferred_element_type=F32
        )
        top, low = 2 * d * N, (2 * d + 1) * N
        stack[top : top + N, :N] = real.astype(BF16)
        stack[top : top + N, N:] = imag.astype(BF16)
        stack[low : low + N, :N] = (-imag).astype(BF16)
        stack[low : low + N, N:] = real.astype(BF16)
    fetch.wait()
    half_product(mixed, stack, send)


def send_half(tau_t, right, mixed):
    vmem = pl.BlockSpec(memory_space=pltpu.VMEM)
    return pl.pallas_call(
        send_kernel,
        out_shape=(
            jax.ShapeDtypeStruct((SNK, 2 * ROWS, 2 * N), BF16),
            jax.ShapeDtypeStruct((DEEP, 2 * N), BF16),
        ),
        in_specs=[vmem] * 5 + [pl.BlockSpec(memory_space=pltpu.HBM)],
        out_specs=(vmem, vmem),
        scratch_shapes=[pltpu.VMEM((2, N, DEEP), BF16), pltpu.SemaphoreType.DMA],
        compiler_params=pltpu.CompilerParams(vmem_limit_bytes=VMEM_CAP),
        cost_estimate=pl.CostEstimate(
            flops=2 * (MOM * 4 + 2 * MOM * 4) * N * N * N,
            bytes_accessed=6 * 2**20,
            transcendentals=0,
        ),
        name="send_half",
    )(tau_t, *right, mixed)


def keep_kernel(mixed_far, stack, out, mixed, arrived):
    fetches = [
        pltpu.make_async_copy(mixed_far.at[2 + n], mixed.at[n], arrived.at[n]) for n in range(2)
    ]
    for fetch in fetches:
        fetch.start()
    parts = []
    for n, fetch in enumerate(fetches):
        fetch.wait()
        part = jnp.dot(mixed[n], stack[...], preferred_element_type=F32)
        parts.append(part.reshape(SNK, ROWS, 2 * N))
    out[...] = jnp.concatenate(parts, 1).astype(out.dtype)


def keep_half(mixed, stack):
    vmem = pl.BlockSpec(memory_space=pltpu.VMEM)
    return pl.pallas_call(
        keep_kernel,
        out_shape=jax.ShapeDtypeStruct((SNK, 2 * ROWS, 2 * N), F32),
        in_specs=[pl.BlockSpec(memory_space=pltpu.HBM), vmem],
        out_specs=vmem,
        scratch_shapes=[pltpu.VMEM((2, N, DEEP), BF16), pltpu.SemaphoreType.DMA((2,))],
        compiler_params=pltpu.CompilerParams(vmem_limit_bytes=VMEM_CAP),
        cost_estimate=pl.CostEstimate(
            flops=2 * 2 * MOM * 4 * N * N * N,
            bytes_accessed=5 * 2**20,
            transcendentals=0,
        ),
        name="keep_half",
    )(mixed, stack)


def device(y, c, x, z):
    return ((y * NC + c) * NX + x % NX) * NZ + z % NZ


def spread(block):
    y = lax.axis_index("y")
    lines = [(a, c, b) for a in range(NY) for c in range(NC) for b in range(NX)]
    own = lax.dynamic_index_in_dim(block, y, 0, keepdims=False)
    turns = [
        (device(b, (c + e) % NC, a, 4 * c), device(a, c, a + b, 4 * c + d))
        for a, c, b in lines
        for e, d in enumerate(POSTS)
    ]
    got = [lax.ppermute(own, ALL, turns)]
    for hops in LINES:
        pairs = [
            (device(a, c, b, 4 * c + post), device(a, c, b, 4 * c + d))
            for a, c, b in lines
            for post, d in zip(POSTS, hops)
        ]
        got.append(lax.ppermute(got[0], ALL, pairs))
    part = functools.reduce(jnp.add, got)
    pieces = {0: part}
    for d in ROUND:
        pieces[d] = lax.ppermute(part, "x", [(i, (i + d) % NX) for i in range(NX)])
    return [pieces[d] for d in range(NX)]


def shards(peram, meson_blocks, edge_left, edge_right, edge_node, edge_weight, weight_table):
    return contract(
        peram,
        meson_blocks,
        (edge_left, edge_right, edge_node, edge_weight, weight_table.T),
    )


def contract(peram, meson_blocks, edges):
    core = lax.axis_index("core")
    by_time = jnp.swapaxes(peram[0], 2, 3)
    tau_t = lax.all_to_all(by_time, ("x", "z"), split_axis=0, concat_axis=0, tiled=True)
    mixed = mix(*edges, meson_blocks)
    right = spread(meson_blocks[0])
    send, stack = send_half(tau_t, right, mixed)
    got = lax.ppermute(send, "core", [(0, 1), (1, 0)])
    keep = keep_half(mixed, stack)
    pair = (keep + got.astype(F32)).astype(BF16)
    times = lax.all_to_all(pair, ("x", "z"), split_axis=0, concat_axis=0, tiled=True)
    one = jnp.sum(times.astype(F32), 0)
    total = one
    for d in range(1, NY):
        total = total + lax.ppermute(one, "y", [(i, (i + d) % NY) for i in range(NY)])
    mine = total.astype(BF16)
    other = lax.ppermute(mine, "core", [(0, 1), (1, 0)])
    halves = jnp.where(core == 0, jnp.stack([mine, other]), jnp.stack([other, mine]))
    halves = halves.reshape(2, 2, ROWS, 2, N)
    return jnp.transpose(halves, (2, 0, 1, 3, 4)).reshape(ROWS, NODES, 2, N)


def solution(mesh):
    fine = Mesh(mesh.devices.reshape(NY, NC, NX, NZ), ALL)
    src, snk = ("y", "core"), ("x", "z")
    edges = P(src, snk, None)
    return jax.shard_map(
        shards,
        mesh=fine,
        in_specs=(
            P(src, None, None, None, snk),
            P(snk, None, None, None, None),
            edges,
            edges,
            edges,
            edges,
            P(),
        ),
        out_specs=P(snk, None, None, None),
        check_vma=False,
    )
```

time: 102 us -> 89 us (0.87)
  waiting for transfers between devices: 11.1 us -> 18.1 us
  blocking collectives: 27.7 us -> 20.8 us
  local copies, waits for them, and re-layouts: 8.12 us -> 1.63 us
  starting transfers between devices: 38.3 us -> 34.4 us
  Pallas kernels: 15.1 us -> 13.1 us
    all_to_all x1, blocking collectives: 27.7 us -> 20.8 us  [contract(): lax.all_to_all(pair, ('x', 'z'), split_axis=0, concat_axis=0, tiled=True)]
    ppermute x11 -> x7, waiting for transfers between devices: 6.28 us -> 13.1 us  [the longest x3 8.43 us: spread(): pieces[d] = lax.ppermute(part, 'x', [(i, (i + d) % NX) for i in range(NX)])]
    unnamed x12 -> x0, local copies, waits for them, and re-layouts: 6.49 us -> none
    pallas_call x3 -> x2, Pallas kernels: 13.3 us -> 9.99 us  [the longest x1 7.3 us: mix(): pl.pallas_call(mix_kernel, grid=(N // CHUNK,), out_shape=jax.ShapeDtypeSt...]
    ppermute x3, starting transfers between devices: 4.35 us -> 1.55 us  [contract(): lax.ppermute(one, 'y', [(i, (i + d) % NY) for i in range(NY)])]
    all_to_all x1, starting transfers between devices: 16.4 us -> 13.8 us  [contract(): lax.all_to_all(by_time, ('x', 'z'), split_axis=0, concat_axis=0, tiled=True)]
    ppermute x11 -> x7, starting transfers between devices: 12.4 us -> 14 us  [the longest x1 7.64 us: spread(): got = [lax.ppermute(own, ALL, turns)]]
    pallas_call x1, Pallas kernels: 1.84 us -> 3.13 us  [send_half(): pl.pallas_call(send_kernel, out_shape=(jax.ShapeDtypeStruct((SNK, 2 * ROW...]
  transfers between devices with their start and end apart: 17 -> 13, of which waited for: 6 -> 8; matrix products, arithmetic and copies ran while one was open for 1% -> 0% of each run, Pallas kernels for 13% -> 11%
where the time goes in v2:
time: 89 us; the launch traced here: 88.6 us
  starting transfers between devices  34.4 us (39%)
  blocking collectives  20.8 us (23%)
  waiting for transfers between devices  18.1 us (20%)
  Pallas kernels  13.1 us (15%)
  local copies, waits for them, and re-layouts  1.63 us (2%)
    all_to_all x1, blocking collectives, contract(): lax.all_to_all(pair, ('x', 'z'), split_axis=0, concat_axis=0, tiled=True)  20.8 us
    all_to_all x1, starting transfers between devices, contract(): lax.all_to_all(by_time, ('x', 'z'), split_axis=0, concat_axis=0, tiled=True)  13.8 us
    ppermute x3, waiting for transfers between devices, spread(): pieces[d] = lax.ppermute(part, 'x', [(i, (i + d) % NX) for i in range(NX)])  8.43 us
    ppermute x1, starting transfers between devices, spread(): got = [lax.ppermute(own, ALL, turns)]  7.64 us
    pallas_call x1, Pallas kernels, mix(): pl.pallas_call(mix_kernel, grid=(N // CHUNK,), out_shape=jax.ShapeDtypeSt...  7.3 us
    ppermute x1, waiting for transfers between devices, spread(): got = [lax.ppermute(own, ALL, turns)]  4.66 us
    ppermute x1, starting transfers between devices, contract(): other = lax.ppermute(mine, 'core', [(0, 1), (1, 0)])  4.54 us
    ppermute x3, waiting for transfers between devices, contract(): lax.ppermute(one, 'y', [(i, (i + d) % NY) for i in range(NY)])  3.82 us
  transfers between devices with their start and end apart: 13, of which 8 were waited for; matrix products, arithmetic and copies ran while one was open for 0% of the time, Pallas kernels for 11%

profile of v2, /device:TPU:1, one launch (start us, length us, event | category | flops | bytes accessed | tf_op | source)
XLA Modules:
  0.0 88.6 jit_solution(744747246865118554)
XLA Ops:
  0.0 1.0 %dynamic-slice_bitcast_fusion = bf16[2,256,256]{2,1,0:T(8,128)(2,1)S(1)} fusion(bf16[1,4,2,256,256]{4,3,2,1,0:T(8,128)(2,1)} %blocks.1, s32[]{:T(128)S(6)} %select_n.14), kind=kLoop, calls=%fused_computation.3 | loop fusion | bytes 524292 | tf_op jit(solution)/shard_map/jit(dynamic_index_in_dim)/squeeze | solution.py:186
  1.0 7.6 %collective-permute-start = (bf16[2,256,256]{2,1,0:T(8,128)(2,1)S(1)}, bf16[2,256,256]{2,1,0:T(8,128)(2,1)S(1)}, u32[]{:S(2)}, u32[]{:S(2)}) collective-permute-start(bf16[2,256,256]{2,1,0:T(8,128)(2,1)S(1)} %dynamic-slice_bitcast_fusion), channel_id=1, source_target_pairs={{0,0},{32,3},{64,8},{96,11},{128,16},{160,19},{192,24},{224,27},{3... | collective-permute-start | bytes 786440 | tf_op jit(solution)/shard_map/ppermute | solution.py:192
  8.6 4.7 %collective-permute-done = bf16[2,256,256]{2,1,0:T(8,128)(2,1)S(1)} collective-permute-done((bf16[2,256,256]{2,1,0:T(8,128)(2,1)S(1)}, bf16[2,256,256]{2,1,0:T(8,128)(2,1)S(1)}, u32[]{:S(2)}, u32[]{:S(2)}) %collective-permute-start) | collective-permute-done | bytes 262176 | tf_op jit(solution)/shard_map/ppermute | solution.py:192
  13.3 1.3 %collective-permute-start.3 = (bf16[2,256,256]{2,1,0:T(8,128)(2,1)S(1)}, bf16[2,256,256]{2,1,0:T(8,128)(2,1)S(1)}, u32[]{:S(2)}, u32[]{:S(2)}) collective-permute-start(bf16[2,256,256]{2,1,0:T(8,128)(2,1)S(1)} %collective-permute-done), channel_id=1, source_target_pairs={{0,1},{3,4},{8,9},{11,12},{16,17},{19,20},{24,25},{27,28},{36,37},... | collective-permute-start | bytes 786440 | tf_op jit(solution)/shard_map/ppermute | solution.py:199
  14.6 0.7 collective-permute-start.2
  15.3 0.7 collective-permute-start.1
  15.9 13.8 %all-to-all-start = ((bf16[32,2,8,256]{3,2,1,0:T(8,128)(2,1)}), bf16[32,2,8,256]{3,2,1,0:T(8,128)(2,1)S(1)}, u32[]{:S(2)}, u32[]{:S(2)}) async-start(bf16[32,2,8,256]{3,2,1,0:T(8,128)(2,1)} %bitcast.9), calls=%async_computation | async-start | bytes 524288 | tf_op jit(solution)/shard_map/all_to_all | solution.py:218
  29.7 0.0 collective-permute-done.3
  29.7 0.0 collective-permute-done.2
  29.8 0.0 collective-permute-done.1
  29.8 0.1 add_add_fusion.r0
  29.8 2.6 %collective-permute-start.6 = (bf16[2,256,256]{2,1,0:T(8,128)(2,1)S(1)}, bf16[2,256,256]{2,1,0:T(8,128)(2,1)S(1)}, u32[]{:S(2)}, u32[]{:S(2)}) collective-permute-start(bf16[2,256,256]{2,1,0:T(8,128)(2,1)S(1)} %add_add_fusion.r0), channel_id=1, source_target_pairs={{0,24},{8,0},{16,8},{24,16},{1,25},{9,1},{17,9},{25,17},{2,26},{10... | collective-permute-start | bytes 786440 | tf_op jit(solution)/shard_map/ppermute | solution.py:203
  32.4 0.5 collective-permute-start.5
  32.9 0.6 collective-permute-start.4
  33.5 7.3 %mix.1.mixed_any.mixed_far = bf16[4,256,2048]{2,1,0:T(8,128)(2,1)} custom-call(s32[1,1,32]{2,1,0:T(1,128)} %left_e.1, s32[1,1,32]{2,1,0:T(1,128)} %right_e.1, s32[1,1,32]{2,1,0:T(1,128)} %node_e.1, s32[1,1,32]{2,1,0:T(1,128)} %weight_e.1, f32[2,16]{1,0:T(2,128)} %bitcast.11, bf16[1,4,2,256,256]{4,3,2,1,0:T(8,128)(2,1)} %blocks.1), custom_call_target="tpu_custom_call" | custom-call | flops 33554432 | bytes 5242880 | tf_op jit(solution)/shard_map/mix/pallas_call | solution.py:79
  40.8 0.3 all-to-all-done.tau_t
  41.2 4.9 %collective-permute-done.6.r3 = bf16[2,256,256]{2,1,0:T(8,128)(2,1)S(1)} collective-permute-done((bf16[2,256,256]{2,1,0:T(8,128)(2,1)S(1)}, bf16[2,256,256]{2,1,0:T(8,128)(2,1)S(1)}, u32[]{:S(2)}, u32[]{:S(2)}) %collective-permute-start.6) | collective-permute-done | bytes 262176 | tf_op jit(solution)/shard_map/ppermute | solution.py:203
  46.1 0.0 collective-permute-done.5.r2
  46.1 3.5 %collective-permute-done.4.r1 = bf16[2,256,256]{2,1,0:T(8,128)(2,1)S(1)} collective-permute-done((bf16[2,256,256]{2,1,0:T(8,128)(2,1)S(1)}, bf16[2,256,256]{2,1,0:T(8,128)(2,1)S(1)}, u32[]{:S(2)}, u32[]{:S(2)}) %collective-permute-start.4) | collective-permute-done | bytes 262176 | tf_op jit(solution)/shard_map/ppermute | solution.py:203
  49.6 3.1 %send_half.1 = (bf16[32,16,512]{2,1,0:T(8,128)(2,1)S(1)}, bf16[2048,512]{1,0:T(8,128)(2,1)S(1)}) custom-call(bf16[32,2,8,256]{3,2,1,0:T(8,128)(2,1)S(1)} %all-to-all-done.tau_t, bf16[2,256,256]{2,1,0:T(8,128)(2,1)S(1)} %add_add_fusion.r0, bf16[2,256,256]{2,1,0:T(8,128)(2,1)S(1)} %collective-permute-done.4.r1, ...), custom_call_target="tpu_custom_call" | custom-call | flops 1610612736 | bytes 6291456 | tf_op jit(solution)/shard_map/send_half/pallas_call | solution.py:128
  52.7 0.6 collective-permute-start.7
  53.3 2.7 %keep_half.1 = f32[32,16,512]{2,1,0:T(8,128)S(1)} custom-call(bf16[4,256,2048]{2,1,0:T(8,128)(2,1)} %mix.1.mixed_any.mixed_far, bf16[2048,512]{1,0:T(8,128)(2,1)S(1)} %get-tuple-element.7.stack), custom_call_target="tpu_custom_call" | custom-call | flops 1073741824 | bytes 5242880 | tf_op jit(solution)/shard_map/keep_half/pallas_call | solution.py:163
  56.0 0.0 collective-permute-done.7
  56.0 0.2 add_convert_fusion
  56.2 20.8 %all_to_all.10 = bf16[32,16,512]{2,1,0:T(8,128)(2,1)S(1)} all-to-all(bf16[32,16,512]{2,1,0:T(8,128)(2,1)S(1)} %add_convert_fusion), channel_id=1, replica_groups=mesh['y'=4,'core'=2,'x'=4,'z'=8] {'x','z'}, dimensions={0} | all-to-all | bytes 1048576 | tf_op jit(solution)/shard_map/all_to_all | solution.py:225
  77.0 0.1 convert_reduce_fusion
  77.1 0.1 collective-permute-start.10
  77.2 1.3 %collective-permute-start.9 = (f32[16,512]{1,0:T(8,128)S(1)}, f32[16,512]{1,0:T(8,128)S(1)}, u32[]{:S(2)}, u32[]{:S(2)}) collective-permute-start(f32[16,512]{1,0:T(8,128)S(1)} %convert_reduce_fusion), channel_id=1, source_target_pairs={{0,128},{64,192},{128,0},{192,64},{1,129},{65,193},{129,1},{193,65... | collective-permute-start | bytes 98312 | tf_op jit(solution)/shard_map/ppermute | solution.py:229
  78.5 0.2 collective-permute-start.8
  78.7 1.3 %collective-permute-done.10 = f32[16,512]{1,0:T(8,128)S(1)} collective-permute-done((f32[16,512]{1,0:T(8,128)S(1)}, f32[16,512]{1,0:T(8,128)S(1)}, u32[]{:S(2)}, u32[]{:S(2)}) %collective-permute-start.10) | collective-permute-done | bytes 32800 | tf_op jit(solution)/shard_map/ppermute | solution.py:229
  80.0 1.6 %collective-permute-done.9 = f32[16,512]{1,0:T(8,128)S(1)} collective-permute-done((f32[16,512]{1,0:T(8,128)S(1)}, f32[16,512]{1,0:T(8,128)S(1)}, u32[]{:S(2)}, u32[]{:S(2)}) %collective-permute-start.9) | collective-permute-done | bytes 32800 | tf_op jit(solution)/shard_map/ppermute | solution.py:229
  81.6 0.9 %collective-permute-done.8 = f32[16,512]{1,0:T(8,128)S(1)} collective-permute-done((f32[16,512]{1,0:T(8,128)S(1)}, f32[16,512]{1,0:T(8,128)S(1)}, u32[]{:S(2)}, u32[]{:S(2)}) %collective-permute-start.8) | collective-permute-done | bytes 32800 | tf_op jit(solution)/shard_map/ppermute | solution.py:229
  82.5 4.5 %collective-permute-start.11 = (bf16[16,512]{1,0:T(8,128)(2,1)S(1)}, bf16[16,512]{1,0:T(8,128)(2,1)S(1)}, u32[]{:S(2)}, u32[]{:S(2)}) collective-permute-start(bf16[16,512]{1,0:T(8,128)(2,1)S(1)} %add_convert_fusion.1), channel_id=1, source_target_pairs={{0,32},{32,0},{1,33},{33,1},{2,34},{34,2},{3,35},{35,3},{4,36},{36... | collective-permute-start | bytes 49160 | tf_op jit(solution)/shard_map/ppermute | solution.py:231
  87.0 0.8 collective-permute-done.11
  87.9 0.1 broadcast_select_fusion
  87.9 0.6 copy.8
  (3 shorter events, 0.0 us)
Async XLA Ops:
  1.0 12.3 %collective-permute-start = (bf16[2,256,256]{2,1,0:T(8,128)(2,1)S(1)}, bf16[2,256,256]{2,1,0:T(8,128)(2,1)S(1)}, u32[]{:S(2)}, u32[]{:S(2)}) collective-permute-start(bf16[2,256,256]{2,1,0:T(8,128)(2,1)S(1)} %dynamic-slice_bitcast_fusion), channel_id=1, source_target_pairs={{0,0},{32,3},{64,8},{96,11},{128,16},{160,19},{192,24},{224,27},{3... | collective-permute-start | bytes 786440 | tf_op jit(solution)/shard_map/ppermute | solution.py:192
  13.3 16.5 %collective-permute-start.3 = (bf16[2,256,256]{2,1,0:T(8,128)(2,1)S(1)}, bf16[2,256,256]{2,1,0:T(8,128)(2,1)S(1)}, u32[]{:S(2)}, u32[]{:S(2)}) collective-permute-start(bf16[2,256,256]{2,1,0:T(8,128)(2,1)S(1)} %collective-permute-done), channel_id=1, source_target_pairs={{0,1},{3,4},{8,9},{11,12},{16,17},{19,20},{24,25},{27,28},{36,37},... | collective-permute-start | bytes 786440 | tf_op jit(solution)/shard_map/ppermute | solution.py:199
  14.6 15.2 %collective-permute-start.2 = (bf16[2,256,256]{2,1,0:T(8,128)(2,1)S(1)}, bf16[2,256,256]{2,1,0:T(8,128)(2,1)S(1)}, u32[]{:S(2)}, u32[]{:S(2)}) collective-permute-start(bf16[2,256,256]{2,1,0:T(8,128)(2,1)S(1)} %collective-permute-done), channel_id=1, source_target_pairs={{0,7},{3,2},{8,15},{11,10},{16,23},{19,18},{24,31},{27,26},{36,35}... | collective-permute-start | bytes 786440 | tf_op jit(solution)/shard_map/ppermute | solution.py:199
  15.3 14.5 %collective-permute-start.1 = (bf16[2,256,256]{2,1,0:T(8,128)(2,1)S(1)}, bf16[2,256,256]{2,1,0:T(8,128)(2,1)S(1)}, u32[]{:S(2)}, u32[]{:S(2)}) collective-permute-start(bf16[2,256,256]{2,1,0:T(8,128)(2,1)S(1)} %collective-permute-done), channel_id=1, source_target_pairs={{0,6},{3,5},{8,14},{11,13},{16,22},{19,21},{24,30},{27,29},{36,34}... | collective-permute-start | bytes 786440 | tf_op jit(solution)/shard_map/ppermute | solution.py:199
  15.9 25.2 %all-to-all-start = ((bf16[32,2,8,256]{3,2,1,0:T(8,128)(2,1)}), bf16[32,2,8,256]{3,2,1,0:T(8,128)(2,1)S(1)}, u32[]{:S(2)}, u32[]{:S(2)}) async-start(bf16[32,2,8,256]{3,2,1,0:T(8,128)(2,1)} %bitcast.9), calls=%async_computation | async-start | bytes 524288 | tf_op jit(solution)/shard_map/all_to_all | solution.py:218
  29.8 16.2 %collective-permute-start.6 = (bf16[2,256,256]{2,1,0:T(8,128)(2,1)S(1)}, bf16[2,256,256]{2,1,0:T(8,128)(2,1)S(1)}, u32[]{:S(2)}, u32[]{:S(2)}) collective-permute-start(bf16[2,256,256]{2,1,0:T(8,128)(2,1)S(1)} %add_add_fusion.r0), channel_id=1, source_target_pairs={{0,24},{8,0},{16,8},{24,16},{1,25},{9,1},{17,9},{25,17},{2,26},{10... | collective-permute-start | bytes 786440 | tf_op jit(solution)/shard_map/ppermute | solution.py:203
  32.4 13.7 %collective-permute-start.5 = (bf16[2,256,256]{2,1,0:T(8,128)(2,1)S(1)}, bf16[2,256,256]{2,1,0:T(8,128)(2,1)S(1)}, u32[]{:S(2)}, u32[]{:S(2)}) collective-permute-start(bf16[2,256,256]{2,1,0:T(8,128)(2,1)S(1)} %add_add_fusion.r0), channel_id=1, source_target_pairs={{0,16},{8,24},{16,0},{24,8},{1,17},{9,25},{17,1},{25,9},{2,18},{10... | collective-permute-start | bytes 786440 | tf_op jit(solution)/shard_map/ppermute | solution.py:203
  32.9 16.7 %collective-permute-start.4 = (bf16[2,256,256]{2,1,0:T(8,128)(2,1)S(1)}, bf16[2,256,256]{2,1,0:T(8,128)(2,1)S(1)}, u32[]{:S(2)}, u32[]{:S(2)}) collective-permute-start(bf16[2,256,256]{2,1,0:T(8,128)(2,1)S(1)} %add_add_fusion.r0), channel_id=1, source_target_pairs={{0,8},{8,16},{16,24},{24,0},{1,9},{9,17},{17,25},{25,1},{2,10},{10... | collective-permute-start | bytes 786440 | tf_op jit(solution)/shard_map/ppermute | solution.py:203
  52.7 3.3 %collective-permute-start.7 = (bf16[32,16,512]{2,1,0:T(8,128)(2,1)S(1)}, bf16[32,16,512]{2,1,0:T(8,128)(2,1)S(1)}, u32[]{:S(2)}, u32[]{:S(2)}) collective-permute-start(bf16[32,16,512]{2,1,0:T(8,128)(2,1)S(1)} %get-tuple-element.8), channel_id=1, source_target_pairs={{0,32},{32,0},{1,33},{33,1},{2,34},{34,2},{3,35},{35,3},{4,36},{36... | collective-permute-start | bytes 1572872 | tf_op jit(solution)/shard_map/ppermute | solution.py:222
  77.1 2.8 %collective-permute-start.10 = (f32[16,512]{1,0:T(8,128)S(1)}, f32[16,512]{1,0:T(8,128)S(1)}, u32[]{:S(2)}, u32[]{:S(2)}) collective-permute-start(f32[16,512]{1,0:T(8,128)S(1)} %convert_reduce_fusion), channel_id=1, source_target_pairs={{0,192},{64,0},{128,64},{192,128},{1,193},{65,1},{129,65},{193,129... | collective-permute-start | bytes 98312 | tf_op jit(solution)/shard_map/ppermute | solution.py:229
  77.2 4.3 %collective-permute-start.9 = (f32[16,512]{1,0:T(8,128)S(1)}, f32[16,512]{1,0:T(8,128)S(1)}, u32[]{:S(2)}, u32[]{:S(2)}) collective-permute-start(f32[16,512]{1,0:T(8,128)S(1)} %convert_reduce_fusion), channel_id=1, source_target_pairs={{0,128},{64,192},{128,0},{192,64},{1,129},{65,193},{129,1},{193,65... | collective-permute-start | bytes 98312 | tf_op jit(solution)/shard_map/ppermute | solution.py:229
  78.5 4.0 %collective-permute-start.8 = (f32[16,512]{1,0:T(8,128)S(1)}, f32[16,512]{1,0:T(8,128)S(1)}, u32[]{:S(2)}, u32[]{:S(2)}) collective-permute-start(f32[16,512]{1,0:T(8,128)S(1)} %convert_reduce_fusion), channel_id=1, source_target_pairs={{0,64},{64,128},{128,192},{192,0},{1,65},{65,129},{129,193},{193,1... | collective-permute-start | bytes 98312 | tf_op jit(solution)/shard_map/ppermute | solution.py:229
  82.5 5.4 %collective-permute-start.11 = (bf16[16,512]{1,0:T(8,128)(2,1)S(1)}, bf16[16,512]{1,0:T(8,128)(2,1)S(1)}, u32[]{:S(2)}, u32[]{:S(2)}) collective-permute-start(bf16[16,512]{1,0:T(8,128)(2,1)S(1)} %add_convert_fusion.1), channel_id=1, source_target_pairs={{0,32},{32,0},{1,33},{33,1},{2,34},{34,2},{3,35},{35,3},{4,36},{36... | collective-permute-start | bytes 49160 | tf_op jit(solution)/shard_map/ppermute | solution.py:231
